TPU v7x, 32 devices: a whole 2x2x4 slice. The times are simulated.
32 devices in a mesh: dom: 8 (over z, x), band: 4 (over y, core).
Axes of the slice: x: 2, y: 2, z: 4, core: 2. Of those that a mesh axis runs over, the one named last changes fastest.
Arguments:
- orbitals: float32 [32, 96, 64, 128], P('band', 'dom'), may hold values from -1400 to 1400
- potential: float32 [96, 64, 128], P('dom'), may hold values from 0.1 to 2
Outputs:
- ortho_orbitals: float32 [32, 96, 64, 128], P('band', 'dom')
All inputs are finite; a program needn't handle non-finite values.
Results may differ from a plain program's by a relative error of at most 0.0003.
Values sent between devices are 32-bit elements; how exact they have to be, the bound alone decides.
A program may use at most 64 MiB of HBM per device.

v0:
```python
import jax
import jax.numpy as jnp
from jax import lax
from jax.sharding import PartitionSpec as P

stencil_weights = [
    -5369.0 / 1800.0,
    12.0 / 7.0,
    -15.0 / 56.0,
    10.0 / 189.0,
    -1.0 / 112.0,
    2.0 / 1925.0,
    -1.0 / 16632.0,
]
center_shift = 9.5
half_width = 7.5


def padded_2(block, sides, width):
    for axis, dim in sides:
        count = lax.axis_size(axis)
        forward = [(i, i + 1) for i in range(count - 1)]
        backward = [(target, source) for source, target in forward]
        low = lax.ppermute(
            lax.slice_in_dim(block, block.shape[dim] - width, None, axis=dim), axis, forward
        )
        high = lax.ppermute(lax.slice_in_dim(block, 0, width, axis=dim), axis, backward)
        block = jnp.concatenate([low, block, high], axis=dim)
    return block


def apply_hamiltonian(padded, field_potential):
    length = field_potential.shape[0]
    inner = padded[:, 6 : 6 + length]
    rows_y = inner.shape[2]
    rows_z = inner.shape[3]
    spread = jnp.pad(inner, ((0, 0), (0, 0), (6, 6), (6, 6)))
    laplace = 3.0 * stencil_weights[0] * inner
    for offset in range(1, 7):
        near = (
            padded[:, 6 + offset : 6 + offset + length]
            + padded[:, 6 - offset : 6 - offset + length]
        )
        near = (
            near
            + spread[:, :, 6 + offset : 6 + offset + rows_y, 6 : 6 + rows_z]
            + spread[:, :, 6 - offset : 6 - offset + rows_y, 6 : 6 + rows_z]
        )
        near = (
            near
            + spread[:, :, 6 : 6 + rows_y, 6 + offset : 6 + offset + rows_z]
            + spread[:, :, 6 : 6 + rows_y, 6 - offset : 6 - offset + rows_z]
        )
        laplace = laplace + stencil_weights[offset] * near
    return -0.5 * laplace + field_potential * inner


def shards(orbitals, potential):
    own_rows = orbitals.shape[1]
    padded = padded_2(orbitals, (("dom", 1),), 6)
    first = (apply_hamiltonian(padded, potential) - center_shift * orbitals) / half_width
    padded_first = padded_2(first, (("dom", 1),), 6)
    filtered = (
        2.0 * (apply_hamiltonian(padded_first, potential) - center_shift * first) / half_width
        - orbitals
    )
    cells = lax.all_to_all(filtered, "band", split_axis=2, concat_axis=0, tiled=True)
    count = cells.shape[0]
    flat = cells.reshape(count, -1)
    partial_correlation = jnp.dot(
        flat, flat.T, precision=lax.Precision.HIGHEST, preferred_element_type=jnp.float32
    )
    all_cells = own_rows * lax.axis_size("dom") * orbitals.shape[2] * orbitals.shape[3]
    correlation = lax.psum(partial_correlation, ("dom", "band")) / jnp.float32(all_cells)
    lower = jnp.linalg.cholesky(correlation)
    inverse = lax.linalg.triangular_solve(
        lower, jnp.eye(count, dtype=correlation.dtype), left_side=True, lower=True
    )
    ortho = jnp.dot(
        inverse, flat, precision=lax.Precision.HIGHEST, preferred_element_type=jnp.float32
    ).reshape(cells.shape)
    return lax.all_to_all(ortho, "band", split_axis=0, concat_axis=2, tiled=True)


def solution(mesh):
    in_specs = (P("band", "dom", None, None), P("dom", None, None))
    out_specs = P("band", "dom", None, None)
    return jax.shard_map(shards, mesh=mesh, in_specs=in_specs, out_specs=out_specs, check_vma=False)
```

profile of v0, /device:TPU:0, one launch (start us, length us, event | category | flops | bytes accessed | tf_op | source)
XLA Modules:
  0.0 322.1 jit_solution(681666642300067285)
XLA Ops:
  0.0 2.2 fusion.103
  2.2 0.0 copy-start
  2.2 5.2 %collective-permute-start.1 = (f32[8,6,64,128]{3,2,1,0:T(8,128)S(1)}, f32[8,6,64,128]{3,2,1,0:T(8,128)S(1)}, u32[]{:S(2)}, u32[]{:S(2)}) collective-permute-start(f32[8,6,64,128]{3,2,1,0:T(8,128)S(1)} %get-tuple-element.10), channel_id=1, source_target_pairs={{0,4},{4,8},{8,12},{12,16},{16,20},{20,24},{24,28},{1,5},{5,9},{9,... | collective-permute-start | bytes 4718600 | tf_op jit(solution)/shard_map/ppermute | solution.py:24
  7.4 1.3 collective-permute-start
  8.7 65.9 %collective-permute-done.1 = f32[8,6,64,128]{3,2,1,0:T(8,128)S(1)} collective-permute-done((f32[8,6,64,128]{3,2,1,0:T(8,128)S(1)}, f32[8,6,64,128]{3,2,1,0:T(8,128)S(1)}, u32[]{:S(2)}, u32[]{:S(2)}) %collective-permute-start.1) | collective-permute-done | bytes 1572896 | tf_op jit(solution)/shard_map/ppermute | solution.py:24
  74.7 0.1 constant_dynamic-update-slice_fusion.3
  74.8 0.0 copy-done
  74.8 0.9 constant_dynamic-update-slice_fusion.1
  75.7 0.0 copy-start.3
  75.8 0.0 collective-permute-done
  75.8 0.2 constant_dynamic-update-slice_fusion
  75.9 0.8 copy-done.3
  76.7 11.5 %broadcast_multiply_fusion = (f32[8,12,64,128]{3,2,1,0:T(8,128)}, f32[8,12,64,128]{3,2,1,0:T(8,128)}) fusion(f32[8,12,64,128]{3,2,1,0:T(8,128)S(1)} %copy-done, f32[12,64,128]{2,1,0:T(8,128)S(1)} %copy-done.3, f32[8,18,64,128]{3,2,1,0:T(8,128)S(1)} %get-tuple-element.12, f32[8,18,64,128]{3,2,1,0:T(8,128)S(1)} %constant_dynamic-update-slice_fusion), kind=kLoop, calls=%fused_computation.175 | loop fusion | flops 38535168 | bytes 47579136 | tf_op jit(solution)/shard_map/div | solution.py:61
  88.2 0.0 copy-start.1
  88.2 0.0 copy-start.2
  88.2 2.3 fusion.102
  90.5 1.4 collective-permute-start.2
  91.9 5.1 %collective-permute-start.3 = (f32[8,6,64,128]{3,2,1,0:T(8,128)S(1)}, f32[8,6,64,128]{3,2,1,0:T(8,128)S(1)}, u32[]{:S(2)}, u32[]{:S(2)}) collective-permute-start(f32[8,6,64,128]{3,2,1,0:T(8,128)S(1)} %get-tuple-element.8), channel_id=1, source_target_pairs={{0,4},{4,8},{8,12},{12,16},{16,20},{20,24},{24,28},{1,5},{5,9},{9,... | collective-permute-start | bytes 4718600 | tf_op jit(solution)/shard_map/ppermute | solution.py:24
  97.1 31.5 %collective-permute-done.2 = f32[8,6,64,128]{3,2,1,0:T(8,128)S(1)} collective-permute-done((f32[8,6,64,128]{3,2,1,0:T(8,128)S(1)}, f32[8,6,64,128]{3,2,1,0:T(8,128)S(1)}, u32[]{:S(2)}, u32[]{:S(2)}) %collective-permute-start.2) | collective-permute-done | bytes 1572896 | tf_op jit(solution)/shard_map/ppermute | solution.py:27
  128.5 33.9 %collective-permute-done.3 = f32[8,6,64,128]{3,2,1,0:T(8,128)S(1)} collective-permute-done((f32[8,6,64,128]{3,2,1,0:T(8,128)S(1)}, f32[8,6,64,128]{3,2,1,0:T(8,128)S(1)}, u32[]{:S(2)}, u32[]{:S(2)}) %collective-permute-start.3) | collective-permute-done | bytes 1572896 | tf_op jit(solution)/shard_map/ppermute | solution.py:24
  162.4 0.0 copy-start.4
  162.4 1.1 copy-done.4
  163.5 0.0 copy-done.1
  163.5 0.0 copy-done.2
  163.5 11.9 %fusion.13 = f32[8,12,64,128]{3,2,1,0:T(8,128)S(1)} fusion(f32[8,12,64,128]{3,2,1,0:T(8,128)S(1)} %copy-done, f32[8,12,64,128]{3,2,1,0:T(8,128)S(1)} %copy-done.1, f32[8,6,64,128]{3,2,1,0:T(8,128)} %copy-done.4, f32[8,6,64,128]{3,2,1,0:T(8,128)S(1)} %collective-permute-done.2, f32[8,12,64,128]{3,2,1,0:T(8,128)S(1)} %copy-done.2, ...), kind=kLoop, calls=%fused_computation.81 | loop fusion | flops 48758784 | bytes 16121856 | tf_op jit(solution)/shard_map/sub | solution.py:64
  175.5 1.8 copy.28
  177.3 39.5 %all_to_all.33 = f32[8,12,64,128]{3,0,1,2:T(8,128)S(1)} all-to-all(f32[8,12,64,128]{3,0,1,2:T(8,128)S(1)} %copy.28), channel_id=1, replica_groups=mesh['dom'=8,'band'=4] {'band'}, dimensions={2} | all-to-all | bytes 6291456 | tf_op jit(solution)/shard_map/all_to_all | solution.py:67
  216.8 3.5 %copy.41 = f32[8,12,4,16,128]{4,3,1,0,2:T(8,128)} copy(f32[8,12,4,16,128]{4,0,1,3,2:T(8,128)S(1)} %bitcast.34) | data formatting | bytes 6291456 | tf_op jit(solution)/shard_map/all_to_all | solution.py:67
  220.3 2.2 reshape.16
  222.5 2.6 fusion.104
  225.1 40.6 %psum.7 = f32[32,32]{0,1:T(8,128)S(1)} all-reduce(f32[32,32]{0,1:T(8,128)S(1)} %fusion.104), channel_id=1, replica_groups=mesh['dom'=8,'band'=4] {'dom','band'}, use_global_device_ids=true, to_apply=%region_0.1 | all-reduce | flops 1024 | bytes 8192 | tf_op jit(solution)/shard_map/psum | solution.py:74
  265.7 0.1 copy.31
  265.8 2.9 cholesky.17
  268.7 0.6 compare_reduce_fusion
  269.4 0.7 fusion.98
  270.0 2.4 custom-call.6
  272.5 0.2 convolution_bitcast_fusion
  272.7 0.6 copy.37
  273.3 4.6 %fusion.96 = f32[32,12,16,128]{3,0,2,1:T(8,128)S(1)} fusion(f32[32,32,1,1]{1,0,3,2:T(8,128)S(1)} %convolution_bitcast_fusion, f32[12,16,128,32]{2,1,0,3:T(8,128)S(1)} %bitcast.33), kind=kOutput, calls=%fused_computation.172 | convolution fusion | flops 301989888 | bytes 6295552 | tf_op jit(solution)/shard_map/dot_general | solution.py:79
  277.9 1.8 copy.33
  279.7 40.3 %all_to_all.34 = f32[32,12,16,128]{3,2,1,0:T(8,128)S(1)} all-to-all(f32[32,12,16,128]{3,2,1,0:T(8,128)S(1)} %copy.33), channel_id=1, replica_groups=mesh['dom'=8,'band'=4] {'band'}, dimensions={0} | all-to-all | bytes 6291456 | tf_op jit(solution)/shard_map/all_to_all | solution.py:82
  320.0 2.1 copy.34
  (4 shorter events, 0.1 us)
Async XLA Ops:
  2.2 72.6 %copy-start = (f32[8,12,64,128]{3,2,1,0:T(8,128)S(1)}, f32[8,12,64,128]{3,2,1,0:T(8,128)}, u32[]{:S(2)}) copy-start(f32[8,12,64,128]{3,2,1,0:T(8,128)} %param.2) | copy-start | bytes 9437188
  2.2 72.5 %collective-permute-start.1 = (f32[8,6,64,128]{3,2,1,0:T(8,128)S(1)}, f32[8,6,64,128]{3,2,1,0:T(8,128)S(1)}, u32[]{:S(2)}, u32[]{:S(2)}) collective-permute-start(f32[8,6,64,128]{3,2,1,0:T(8,128)S(1)} %get-tuple-element.10), channel_id=1, source_target_pairs={{0,4},{4,8},{8,12},{12,16},{16,20},{20,24},{24,28},{1,5},{5,9},{9,... | collective-permute-start | bytes 4718600 | tf_op jit(solution)/shard_map/ppermute | solution.py:24
  7.4 68.3 %collective-permute-start = (f32[8,6,64,128]{3,2,1,0:T(8,128)S(1)}, f32[8,6,64,128]{3,2,1,0:T(8,128)S(1)}, u32[]{:S(2)}, u32[]{:S(2)}) collective-permute-start(f32[8,6,64,128]{3,2,1,0:T(8,128)S(1)} %get-tuple-element.9), channel_id=1, source_target_pairs={{4,0},{8,4},{12,8},{16,12},{20,16},{24,20},{28,24},{5,1},{9,5},{13... | collective-permute-start | bytes 4718600 | tf_op jit(solution)/shard_map/ppermute | solution.py:27
  75.7 1.0 copy-start.3
  88.2 75.3 %copy-start.1 = (f32[8,12,64,128]{3,2,1,0:T(8,128)S(1)}, f32[8,12,64,128]{3,2,1,0:T(8,128)}, u32[]{:S(2)}) copy-start(f32[8,12,64,128]{3,2,1,0:T(8,128)} %get-tuple-element.5) | copy-start | bytes 9437188
  88.2 75.3 %copy-start.2 = (f32[8,12,64,128]{3,2,1,0:T(8,128)S(1)}, f32[8,12,64,128]{3,2,1,0:T(8,128)}, u32[]{:S(2)}) copy-start(f32[8,12,64,128]{3,2,1,0:T(8,128)} %get-tuple-element.6) | copy-start | bytes 9437188
  90.5 38.1 %collective-permute-start.2 = (f32[8,6,64,128]{3,2,1,0:T(8,128)S(1)}, f32[8,6,64,128]{3,2,1,0:T(8,128)S(1)}, u32[]{:S(2)}, u32[]{:S(2)}) collective-permute-start(f32[8,6,64,128]{3,2,1,0:T(8,128)S(1)} %get-tuple-element.7), channel_id=1, source_target_pairs={{4,0},{8,4},{12,8},{16,12},{20,16},{24,20},{28,24},{5,1},{9,5},{13... | collective-permute-start | bytes 4718600 | tf_op jit(solution)/shard_map/ppermute | solution.py:27
  91.9 70.5 %collective-permute-start.3 = (f32[8,6,64,128]{3,2,1,0:T(8,128)S(1)}, f32[8,6,64,128]{3,2,1,0:T(8,128)S(1)}, u32[]{:S(2)}, u32[]{:S(2)}) collective-permute-start(f32[8,6,64,128]{3,2,1,0:T(8,128)S(1)} %get-tuple-element.8), channel_id=1, source_target_pairs={{0,4},{4,8},{8,12},{12,16},{16,20},{20,24},{24,28},{1,5},{5,9},{9,... | collective-permute-start | bytes 4718600 | tf_op jit(solution)/shard_map/ppermute | solution.py:24
  162.4 1.1 copy-start.4
where the time goes:
time: 323 us; the launch traced here: 322 us
  waiting for transfers between devices  131 us (41%)
  blocking collectives  120 us (37%)
  other arithmetic  30.1 us (9%)
  local copies, waits for them, and re-layouts  19.7 us (6%)
  starting transfers between devices  13.1 us (4%)
  matrix products  7.36 us (2%)
    ppermute x2, waiting for transfers between devices, padded_2(): lax.ppermute(lax.slice_in_dim(block, block.shape[dim] - width, None, axis...  99.8 us
    psum x1, blocking collectives, shards(): lax.psum(partial_correlation, ('dom', 'band')) / jnp.float32(all_cells)  40.6 us
    all_to_all x1, blocking collectives, shards(): lax.all_to_all(ortho, 'band', split_axis=0, concat_axis=2, tiled=True)  40.3 us
    all_to_all x1, blocking collectives, shards(): lax.all_to_all(filtered, 'band', split_axis=2, concat_axis=0, tiled=True)  39.5 us
    ppermute x2, waiting for transfers between devices, padded_2(): lax.ppermute(lax.slice_in_dim(block, 0, width, axis=dim), axis, backward)  31.5 us
    sub x1, other arithmetic, shards(): 2.0 * (apply_hamiltonian(padded_first, potential) - center_shift * first)  11.9 us
    div x1, other arithmetic, shards(): (apply_hamiltonian(padded, potential) - center_shift * orbitals) / half_w...  11.5 us
    ppermute x2, starting transfers between devices, padded_2(): lax.ppermute(lax.slice_in_dim(block, block.shape[dim] - width, None, axis...  10.3 us
  transfers between devices with their start and end apart: 4, of which 3 were waited for; matrix products, arithmetic and copies ran while one was open for 0% of the time, Pallas kernels for 0%

commit v1 on v0

--- a/solution.py
+++ b/solution.py
@@ -1,3 +1,4 @@
+import functools
 import jax
 import jax.numpy as jnp
 from jax import lax
@@ -14,6 +15,14 @@
 ]
 center_shift = 9.5
 half_width = 7.5
+
+
+def supply_all_numbers(frame_in, a_name):
+    w_next = lax.all_gather(frame_in, axis_name=a_name)
+    return jnp.sum(w_next, axis=0)
+
+
+show_the_pools = functools.partial(supply_all_numbers, a_name=("dom", "band"))
 
 
 def padded_2(block, sides, width):
@@ -71,7 +80,7 @@
         flat, flat.T, precision=lax.Precision.HIGHEST, preferred_element_type=jnp.float32
     )
     all_cells = own_rows * lax.axis_size("dom") * orbitals.shape[2] * orbitals.shape[3]
-    correlation = lax.psum(partial_correlation, ("dom", "band")) / jnp.float32(all_cells)
+    correlation = show_the_pools(partial_correlation) / jnp.float32(all_cells)
     lower = jnp.linalg.cholesky(correlation)
     inverse = lax.linalg.triangular_solve(
         lower, jnp.eye(count, dtype=correlation.dtype), left_side=True, lower=True

time: 323 us -> 325 us (level)
    all_gather x0 -> x1, blocking collectives: none -> 43.2 us  [supply_all_numbers(): w_next = lax.all_gather(frame_in, axis_name=a_name)]
    psum x1 -> x0, blocking collectives: 40.6 us -> none  [shards(): lax.psum(partial_correlation, ('dom', 'band')) / jnp.float32(all_cells)]
where the time goes in v1:
time: 325 us
  waiting for transfers between devices  131 us (40%)
  blocking collectives  122 us (38%)
  other arithmetic  31.2 us (10%)
  local copies, waits for them, and re-layouts  19.8 us (6%)
  starting transfers between devices  13.1 us (4%)
  matrix products  7.36 us (2%)
    ppermute x2, waiting for transfers between devices, padded_2(): lax.ppermute(lax.slice_in_dim(block, block.shape[dim] - width, None, axis...  99.8 us
    all_gather x1, blocking collectives, supply_all_numbers(): w_next = lax.all_gather(frame_in, axis_name=a_name)  43.2 us
    all_to_all x1, blocking collectives, shards(): lax.all_to_all(filtered, 'band', split_axis=2, concat_axis=0, tiled=True)  39.5 us
    all_to_all x1, blocking collectives, shards(): lax.all_to_all(ortho, 'band', split_axis=0, concat_axis=2, tiled=True)  39.4 us
    ppermute x2, waiting for transfers between devices, padded_2(): lax.ppermute(lax.slice_in_dim(block, 0, width, axis=dim), axis, backward)  31.5 us
    sub x1, other arithmetic, shards(): 2.0 * (apply_hamiltonian(padded_first, potential) - center_shift * first)  11.9 us
    div x1, other arithmetic, shards(): (apply_hamiltonian(padded, potential) - center_shift * orbitals) / half_w...  11.5 us
    ppermute x2, starting transfers between devices, padded_2(): lax.ppermute(lax.slice_in_dim(block, block.shape[dim] - width, None, axis...  10.3 us
  transfers between devices with their start and end apart: 4, of which 3 were waited for; matrix products, arithmetic and copies ran while one was open for 0% of the time, Pallas kernels for 0%

profile of v1, /device:TPU:0, one launch (start us, length us, event | category | flops | bytes accessed | tf_op | source)
XLA Modules:
  0.0 325.0 jit_solution(18360705173210993309)
XLA Ops:
  0.0 2.2 fusion.103
  2.2 0.0 copy-start
  2.2 5.2 %collective-permute-start.1 = (f32[8,6,64,128]{3,2,1,0:T(8,128)S(1)}, f32[8,6,64,128]{3,2,1,0:T(8,128)S(1)}, u32[]{:S(2)}, u32[]{:S(2)}) collective-permute-start(f32[8,6,64,128]{3,2,1,0:T(8,128)S(1)} %get-tuple-element.10), channel_id=1, source_target_pairs={{0,4},{4,8},{8,12},{12,16},{16,20},{20,24},{24,28},{1,5},{5,9},{9,... | collective-permute-start | bytes 4718600 | tf_op jit(solution)/shard_map/ppermute | solution.py:33
  7.4 1.3 collective-permute-start
  8.7 65.9 %collective-permute-done.1 = f32[8,6,64,128]{3,2,1,0:T(8,128)S(1)} collective-permute-done((f32[8,6,64,128]{3,2,1,0:T(8,128)S(1)}, f32[8,6,64,128]{3,2,1,0:T(8,128)S(1)}, u32[]{:S(2)}, u32[]{:S(2)}) %collective-permute-start.1) | collective-permute-done | bytes 1572896 | tf_op jit(solution)/shard_map/ppermute | solution.py:33
  74.7 0.1 constant_dynamic-update-slice_fusion.3
  74.8 0.0 copy-done
  74.8 0.9 constant_dynamic-update-slice_fusion.1
  75.7 0.0 copy-start.3
  75.8 0.0 collective-permute-done
  75.8 0.2 constant_dynamic-update-slice_fusion
  75.9 0.8 copy-done.3
  76.7 11.5 %broadcast_multiply_fusion = (f32[8,12,64,128]{3,2,1,0:T(8,128)}, f32[8,12,64,128]{3,2,1,0:T(8,128)}) fusion(f32[8,12,64,128]{3,2,1,0:T(8,128)S(1)} %copy-done, f32[12,64,128]{2,1,0:T(8,128)S(1)} %copy-done.3, f32[8,18,64,128]{3,2,1,0:T(8,128)S(1)} %get-tuple-element.12, f32[8,18,64,128]{3,2,1,0:T(8,128)S(1)} %constant_dynamic-update-slice_fusion), kind=kLoop, calls=%fused_computation.175 | loop fusion | flops 38535168 | bytes 47579136 | tf_op jit(solution)/shard_map/div | solution.py:70
  88.2 0.0 copy-start.1
  88.2 0.0 copy-start.2
  88.2 2.3 fusion.102
  90.5 1.4 collective-permute-start.2
  91.9 5.1 %collective-permute-start.3 = (f32[8,6,64,128]{3,2,1,0:T(8,128)S(1)}, f32[8,6,64,128]{3,2,1,0:T(8,128)S(1)}, u32[]{:S(2)}, u32[]{:S(2)}) collective-permute-start(f32[8,6,64,128]{3,2,1,0:T(8,128)S(1)} %get-tuple-element.8), channel_id=1, source_target_pairs={{0,4},{4,8},{8,12},{12,16},{16,20},{20,24},{24,28},{1,5},{5,9},{9,... | collective-permute-start | bytes 4718600 | tf_op jit(solution)/shard_map/ppermute | solution.py:33
  97.1 31.5 %collective-permute-done.2 = f32[8,6,64,128]{3,2,1,0:T(8,128)S(1)} collective-permute-done((f32[8,6,64,128]{3,2,1,0:T(8,128)S(1)}, f32[8,6,64,128]{3,2,1,0:T(8,128)S(1)}, u32[]{:S(2)}, u32[]{:S(2)}) %collective-permute-start.2) | collective-permute-done | bytes 1572896 | tf_op jit(solution)/shard_map/ppermute | solution.py:36
  128.5 33.9 %collective-permute-done.3 = f32[8,6,64,128]{3,2,1,0:T(8,128)S(1)} collective-permute-done((f32[8,6,64,128]{3,2,1,0:T(8,128)S(1)}, f32[8,6,64,128]{3,2,1,0:T(8,128)S(1)}, u32[]{:S(2)}, u32[]{:S(2)}) %collective-permute-start.3) | collective-permute-done | bytes 1572896 | tf_op jit(solution)/shard_map/ppermute | solution.py:33
  162.4 0.0 copy-start.4
  162.4 1.1 copy-done.4
  163.5 0.0 copy-done.1
  163.5 0.0 copy-done.2
  163.5 11.9 %fusion.13 = f32[8,12,64,128]{3,2,1,0:T(8,128)S(1)} fusion(f32[8,12,64,128]{3,2,1,0:T(8,128)S(1)} %copy-done, f32[8,12,64,128]{3,2,1,0:T(8,128)S(1)} %copy-done.1, f32[8,6,64,128]{3,2,1,0:T(8,128)} %copy-done.4, f32[8,6,64,128]{3,2,1,0:T(8,128)S(1)} %collective-permute-done.2, f32[8,12,64,128]{3,2,1,0:T(8,128)S(1)} %copy-done.2, ...), kind=kLoop, calls=%fused_computation.81 | loop fusion | flops 48758784 | bytes 16121856 | tf_op jit(solution)/shard_map/sub | solution.py:73
  175.5 1.8 copy.26
  177.3 39.5 %all_to_all.33 = f32[8,12,64,128]{3,0,1,2:T(8,128)S(1)} all-to-all(f32[8,12,64,128]{3,0,1,2:T(8,128)S(1)} %copy.26), channel_id=1, replica_groups=mesh['dom'=8,'band'=4] {'band'}, dimensions={2} | all-to-all | bytes 6291456 | tf_op jit(solution)/shard_map/all_to_all | solution.py:76
  216.8 3.5 %copy.38 = f32[8,12,4,16,128]{4,3,1,0,2:T(8,128)} copy(f32[8,12,4,16,128]{4,0,1,3,2:T(8,128)S(1)} %bitcast.35) | data formatting | bytes 6291456 | tf_op jit(solution)/shard_map/all_to_all | solution.py:76
  220.3 2.2 reshape.16
  222.5 2.6 fusion.104
  225.1 43.2 %all-gather = f32[1024,32]{1,0:T(8,128)} all-gather(f32[32,32]{1,0:T(8,128)S(1)} %fusion.104), channel_id=2, replica_groups=mesh['dom'=8,'band'=4] {'dom','band'}, dimensions={0}, use_global_device_ids=true | all-gather | bytes 135168 | tf_op jit(solution)/shard_map/all_gather | solution.py:21
  268.3 1.1 reduce_sum.9
  269.4 0.1 copy.28
  269.5 0.1 copy.29
  269.5 2.9 cholesky.17
  272.5 0.6 compare_reduce_fusion
  273.1 0.7 fusion.98
  273.8 2.4 custom-call.6
  276.2 0.2 convolution_bitcast_fusion
  276.5 0.6 copy.34
  277.0 4.6 %fusion.96 = f32[32,12,16,128]{3,0,2,1:T(8,128)S(1)} fusion(f32[32,32,1,1]{1,0,3,2:T(8,128)S(1)} %convolution_bitcast_fusion, f32[12,16,128,32]{2,1,0,3:T(8,128)S(1)} %bitcast.34), kind=kOutput, calls=%fused_computation.172 | convolution fusion | flops 301989888 | bytes 6295552 | tf_op jit(solution)/shard_map/dot_general | solution.py:88
  281.6 1.8 copy.31
  283.4 39.4 %all_to_all.34 = f32[32,12,16,128]{3,2,1,0:T(8,128)S(1)} all-to-all(f32[32,12,16,128]{3,2,1,0:T(8,128)S(1)} %copy.31), channel_id=1, replica_groups=mesh['dom'=8,'band'=4] {'band'}, dimensions={0} | all-to-all | bytes 6291456 | tf_op jit(solution)/shard_map/all_to_all | solution.py:91
  322.9 2.1 copy.32
  (4 shorter events, 0.1 us)
Async XLA Ops:
  2.2 72.6 %copy-start = (f32[8,12,64,128]{3,2,1,0:T(8,128)S(1)}, f32[8,12,64,128]{3,2,1,0:T(8,128)}, u32[]{:S(2)}) copy-start(f32[8,12,64,128]{3,2,1,0:T(8,128)} %param.2) | copy-start | bytes 9437188
  2.2 72.5 %collective-permute-start.1 = (f32[8,6,64,128]{3,2,1,0:T(8,128)S(1)}, f32[8,6,64,128]{3,2,1,0:T(8,128)S(1)}, u32[]{:S(2)}, u32[]{:S(2)}) collective-permute-start(f32[8,6,64,128]{3,2,1,0:T(8,128)S(1)} %get-tuple-element.10), channel_id=1, source_target_pairs={{0,4},{4,8},{8,12},{12,16},{16,20},{20,24},{24,28},{1,5},{5,9},{9,... | collective-permute-start | bytes 4718600 | tf_op jit(solution)/shard_map/ppermute | solution.py:33
  7.4 68.3 %collective-permute-start = (f32[8,6,64,128]{3,2,1,0:T(8,128)S(1)}, f32[8,6,64,128]{3,2,1,0:T(8,128)S(1)}, u32[]{:S(2)}, u32[]{:S(2)}) collective-permute-start(f32[8,6,64,128]{3,2,1,0:T(8,128)S(1)} %get-tuple-element.9), channel_id=1, source_target_pairs={{4,0},{8,4},{12,8},{16,12},{20,16},{24,20},{28,24},{5,1},{9,5},{13... | collective-permute-start | bytes 4718600 | tf_op jit(solution)/shard_map/ppermute | solution.py:36
  75.7 1.0 copy-start.3
  88.2 75.3 %copy-start.1 = (f32[8,12,64,128]{3,2,1,0:T(8,128)S(1)}, f32[8,12,64,128]{3,2,1,0:T(8,128)}, u32[]{:S(2)}) copy-start(f32[8,12,64,128]{3,2,1,0:T(8,128)} %get-tuple-element.5) | copy-start | bytes 9437188
  88.2 75.3 %copy-start.2 = (f32[8,12,64,128]{3,2,1,0:T(8,128)S(1)}, f32[8,12,64,128]{3,2,1,0:T(8,128)}, u32[]{:S(2)}) copy-start(f32[8,12,64,128]{3,2,1,0:T(8,128)} %get-tuple-element.6) | copy-start | bytes 9437188
  90.5 38.1 %collective-permute-start.2 = (f32[8,6,64,128]{3,2,1,0:T(8,128)S(1)}, f32[8,6,64,128]{3,2,1,0:T(8,128)S(1)}, u32[]{:S(2)}, u32[]{:S(2)}) collective-permute-start(f32[8,6,64,128]{3,2,1,0:T(8,128)S(1)} %get-tuple-element.7), channel_id=1, source_target_pairs={{4,0},{8,4},{12,8},{16,12},{20,16},{24,20},{28,24},{5,1},{9,5},{13... | collective-permute-start | bytes 4718600 | tf_op jit(solution)/shard_map/ppermute | solution.py:36
  91.9 70.5 %collective-permute-start.3 = (f32[8,6,64,128]{3,2,1,0:T(8,128)S(1)}, f32[8,6,64,128]{3,2,1,0:T(8,128)S(1)}, u32[]{:S(2)}, u32[]{:S(2)}) collective-permute-start(f32[8,6,64,128]{3,2,1,0:T(8,128)S(1)} %get-tuple-element.8), channel_id=1, source_target_pairs={{0,4},{4,8},{8,12},{12,16},{16,20},{20,24},{24,28},{1,5},{5,9},{9,... | collective-permute-start | bytes 4718600 | tf_op jit(solution)/shard_map/ppermute | solution.py:33
  162.4 1.1 copy-start.4
